TPU v7x, 32 devices: a whole 2x2x4 slice. The times are simulated.
32 devices in a mesh: row: 4 (over y, x), col: 8 (over z, core).
Axes of the slice: x: 2, y: 2, z: 4, core: 2. Of those that a mesh axis runs over, the one named last changes fastest.
Arguments:
- tokens: bfloat16 [16384, 1024], P(('row', 'col')), may hold values from -6 to 6
- blocks: int32 [16384], P(('row', 'col')), may hold values from 0 to 127, never falling along the last dimension, each value on 1 to 256 neighbouring positions
- w_qkv: bfloat16 [1024, 3, 1024], P('row', None, 'col'), may hold values from -0.25 to 0.25
- b_qv: bfloat16 [2, 1024], P(None, 'col'), may hold values from -1.5 to 1.5
- w_out: bfloat16 [1024, 1024], P('col', 'row'), may hold values from -0.5 to 0.5
- b_out: bfloat16 [1024], replicated, may hold values from -3 to 3
- w_up: bfloat16 [4096, 1024], P('col', 'row'), may hold values from -0.1875 to 0.1875
- b_up: bfloat16 [4096], P('col'), may hold values from -3 to 3
- w_down: bfloat16 [4096, 1024], P('col', 'row'), may hold values from -0.09375 to 0.09375
- b_down: bfloat16 [1024], replicated, may hold values from -3 to 3
- gain1: bfloat16 [1024], replicated, may hold values from 0.5 to 1.5
- shift1: bfloat16 [1024], replicated, may hold values from -1.5 to 1.5
- gain2: bfloat16 [1024], replicated, may hold values from 0.5 to 1.5
- shift2: bfloat16 [1024], replicated, may hold values from -1.5 to 1.5
- grad_out: bfloat16 [16384, 1024], P(('row', 'col')), may hold values from -9 to 9
Outputs:
- output: bfloat16 [16384, 1024], P(('row', 'col'))
- grad_tokens: float32 [16384, 1024], P(('row', 'col'))
- grad_w_qkv: float32 [1024, 3, 1024], P('row', None, 'col')
- grad_b_qv: float32 [2, 1024], P(None, 'col')
- grad_w_out: float32 [1024, 1024], P('col', 'row')
- grad_b_out: float32 [1024], replicated
- grad_w_up: float32 [4096, 1024], P('col', 'row')
- grad_b_up: float32 [4096], P('col')
- grad_w_down: float32 [4096, 1024], P('col', 'row')
- grad_b_down: float32 [1024], replicated
- grad_gain1: float32 [1024], replicated
- grad_shift1: float32 [1024], replicated
- grad_gain2: float32 [1024], replicated
- grad_shift2: float32 [1024], replicated
Inputs may be any that keep to these rules, and one draw needn't show every extreme that they name: `blocks`: block indices never fall along the tokens and every index from the least to the largest occurs; each block holds 1 to 256 tokens, and one holds exactly 256. A block may run across the end of a sequence.
All inputs are finite; a program needn't handle non-finite values.
Results may differ from a plain program's by a relative error of at most 0.012.
The roundings to bfloat16 on the way count: a program that leaves them out, or rounds other values in their place, can miss the bound.
Values may be sent and summed in bfloat16 or wider, within the bound.
A program may use at most 256 MiB of HBM per device.

v0:
```python
import jax
import jax.numpy as jnp
from jax import lax
from jax.sharding import PartitionSpec as P

HD = 64
SEQ_LEN = 4096
EPS = 1e-05


def norm(values_in, gain, shift):
    center = jnp.mean(values_in, axis=-1, keepdims=True)
    centered = values_in - center
    spread = jnp.mean(centered * centered, axis=-1, keepdims=True)
    return centered * lax.rsqrt(spread + EPS) * gain + shift


def gelu_tanh(values_in):
    return jax.nn.gelu(values_in, approximate=True)


def gather_tokens(rows_in):
    return lax.all_gather(rows_in, "col", axis=0, tiled=True)


def sum_tokens(term_fn, local_rows):
    return lax.psum_scatter(
        term_fn(jnp.int32(0), lax.axis_size("col") * local_rows),
        "col",
        scatter_dimension=0,
        tiled=True,
    )


def body(
    tokens,
    blocks,
    w_qkv,
    b_qv,
    w_out,
    b_out,
    w_up,
    b_up,
    w_down,
    b_down,
    gain1,
    shift1,
    gain2,
    shift2,
    grad_out,
):
    f32 = jnp.float32
    bf16 = jnp.bfloat16
    local_rows = tokens.shape[0]
    model_width = tokens.shape[1]
    col_count = lax.axis_size("col")
    group_rows = local_rows * col_count
    head_cols = w_qkv.shape[2]
    heads_here = head_cols // HD
    score_scale = HD ** (-0.5)
    query_rows = min(512, SEQ_LEN)
    block_count = group_rows // query_rows
    qkv_weight = lax.all_gather(w_qkv, "row", axis=0, tiled=True)
    qkv_flat = qkv_weight.reshape(model_width, 3 * head_cols)
    out_weight, down_weight, up_weight = (
        lax.all_gather(w_out, "row", axis=1, tiled=True),
        lax.all_gather(w_down, "row", axis=1, tiled=True),
        lax.all_gather(w_up, "row", axis=1, tiled=True),
    )
    tokens_f = tokens.astype(f32)
    normed_in, norm1_back = jax.vjp(norm, tokens_f, gain1.astype(f32), shift1.astype(f32))
    attn_input = normed_in.astype(bf16)
    attn_rows, block_ids = (
        lax.all_gather(attn_input, "col", axis=0, tiled=True),
        lax.all_gather(blocks, "col", axis=0, tiled=True),
    )
    bias_qv = b_qv.astype(f32)
    mixed = jnp.dot(attn_rows, qkv_flat, preferred_element_type=f32).reshape(
        group_rows, 3, head_cols
    )
    queries = (mixed[:, 0] + bias_qv[0]).astype(bf16).reshape(group_rows, heads_here, HD)
    keys = mixed[:, 1].astype(bf16).reshape(group_rows, heads_here, HD)
    values = (mixed[:, 2] + bias_qv[1]).astype(bf16).reshape(group_rows, heads_here, HD)

    def block_scores(row_start):
        seq_start = row_start // SEQ_LEN * SEQ_LEN
        query_part = lax.dynamic_slice_in_dim(queries, row_start, query_rows, 0)
        key_seq = lax.dynamic_slice_in_dim(keys, seq_start, SEQ_LEN, 0)
        query_blocks = lax.dynamic_slice_in_dim(block_ids, row_start, query_rows, 0)
        key_blocks = lax.dynamic_slice_in_dim(block_ids, seq_start, SEQ_LEN, 0)
        raw_scores = jnp.einsum("qhd,khd->hqk", query_part, key_seq, preferred_element_type=f32)
        allowed = query_blocks[:, None] >= key_blocks[None, :]
        scores = jnp.where(allowed[None], raw_scores * score_scale, -1e30)
        return (scores, query_part, key_seq, seq_start)

    def forward_block(block_index):
        row_start = block_index * query_rows
        scores, query_part, key_seq, seq_start = block_scores(row_start)
        value_seq = lax.dynamic_slice_in_dim(values, seq_start, SEQ_LEN, 0)
        row_max = jnp.max(scores, axis=-1, keepdims=True)
        row_total = jnp.sum(jnp.exp(scores - row_max), axis=-1, keepdims=True)
        log_total = row_max + jnp.log(row_total)
        probs_low = jnp.exp(scores - log_total).astype(bf16)
        block_out = jnp.einsum("hqk,khd->qhd", probs_low, value_seq, preferred_element_type=f32)
        return (block_out, log_total)

    block_outs, log_totals = lax.map(forward_block, jnp.arange(block_count, dtype=jnp.int32))
    heads_out = block_outs.reshape(group_rows, head_cols).astype(bf16)
    part = heads_out
    attn_branch = lax.psum_scatter(
        jnp.dot(part, out_weight, preferred_element_type=f32),
        "col",
        scatter_dimension=0,
        tiled=True,
    )
    resid = tokens_f + attn_branch + b_out.astype(f32)
    normed_mid, norm2_back = jax.vjp(norm, resid, gain2.astype(f32), shift2.astype(f32))
    ffn_input = normed_mid.astype(bf16)
    up_all, down_all, up_bias = (up_weight, down_weight, b_up)
    ffn_rows = gather_tokens(ffn_input)
    up_pre = jnp.einsum("td,fd->tf", ffn_rows, up_all, preferred_element_type=f32) + up_bias.astype(
        f32
    )
    hidden_f, gelu_back = jax.vjp(gelu_tanh, up_pre)
    hidden = hidden_f.astype(bf16)
    part = hidden
    ffn_branch = lax.psum_scatter(
        jnp.dot(part, down_all, preferred_element_type=f32).astype(jnp.bfloat16),
        "col",
        scatter_dimension=0,
        tiled=True,
    ).astype(jnp.float32)
    output = (resid + ffn_branch + b_down.astype(f32)).astype(bf16)
    grad_f = grad_out.astype(f32)
    grad_bdown = jnp.sum(grad_f, axis=0)
    grad_rows = gather_tokens(grad_out)
    grad_wdown = jnp.einsum("tf,td->fd", hidden, grad_rows, preferred_element_type=f32)
    d_hidden = jnp.einsum("td,fd->tf", grad_rows, down_all, preferred_element_type=f32)
    d_up = gelu_back(d_hidden)[0]
    grad_bup = jnp.sum(d_up, axis=0)
    d_up_low = d_up.astype(bf16)
    grad_wup = jnp.einsum("tf,td->fd", d_up_low, ffn_rows, preferred_element_type=f32)

    def up_term(row_start, count):
        return jnp.dot(d_up_low, up_all, preferred_element_type=f32)

    d_norm2 = sum_tokens(up_term, local_rows)
    d_resid_in, grad_gain2, grad_shift2 = norm2_back(d_norm2)
    d_resid = grad_f + d_resid_in
    grad_bout = jnp.sum(d_resid, axis=0)
    d_resid_low = d_resid.astype(bf16)
    resid_rows = gather_tokens(d_resid_low)
    grad_wout = jnp.einsum("tk,td->kd", heads_out, resid_rows, preferred_element_type=f32)
    d_heads = jnp.einsum("td,kd->tk", resid_rows, out_weight, preferred_element_type=f32).astype(
        bf16
    )
    d_heads = d_heads.reshape(group_rows, heads_here, HD)

    def backward_block(carry, block_index):
        grad_keys, grad_values = carry
        row_start = block_index * query_rows
        scores, query_part, key_seq, seq_start = block_scores(row_start)
        value_seq = lax.dynamic_slice_in_dim(values, seq_start, SEQ_LEN, 0)
        probs = jnp.exp(scores - log_totals[block_index])
        probs_low = probs.astype(bf16)
        dout_part = lax.dynamic_slice_in_dim(d_heads, row_start, query_rows, 0)
        value_part = jnp.einsum("hqk,qhd->khd", probs_low, dout_part, preferred_element_type=f32)
        d_probs = jnp.einsum("qhd,khd->hqk", dout_part, value_seq, preferred_element_type=f32)
        d_scores = probs * (d_probs - jnp.sum(probs * d_probs, axis=-1, keepdims=True))
        d_scores_low = d_scores.astype(bf16)
        query_grad = (
            jnp.einsum("hqk,khd->qhd", d_scores_low, key_seq, preferred_element_type=f32)
            * score_scale
        )
        key_part = (
            jnp.einsum("hqk,qhd->khd", d_scores_low, query_part, preferred_element_type=f32)
            * score_scale
        )
        old_keys = lax.dynamic_slice_in_dim(grad_keys, seq_start, SEQ_LEN, 0)
        grad_keys = lax.dynamic_update_slice_in_dim(grad_keys, old_keys + key_part, seq_start, 0)
        old_values = lax.dynamic_slice_in_dim(grad_values, seq_start, SEQ_LEN, 0)
        grad_values = lax.dynamic_update_slice_in_dim(
            grad_values, old_values + value_part, seq_start, 0
        )
        return ((grad_keys, grad_values), query_grad)

    empty = jnp.zeros((group_rows, heads_here, HD), f32)
    (grad_keys, grad_values), grad_queries = lax.scan(
        backward_block, (empty, empty), jnp.arange(block_count, dtype=jnp.int32)
    )
    grad_queries = grad_queries.reshape(group_rows, head_cols)
    grad_keys = grad_keys.reshape(group_rows, head_cols)
    grad_values = grad_values.reshape(group_rows, head_cols)
    grad_bqv = jnp.stack([jnp.sum(grad_queries, axis=0), jnp.sum(grad_values, axis=0)])
    d_mixed = jnp.stack([grad_queries, grad_keys, grad_values], axis=1).astype(bf16)
    d_mixed_flat = d_mixed.reshape(group_rows, 3 * head_cols)
    grad_wqkv = jnp.einsum(
        "td,tk->dk", attn_rows, d_mixed_flat, preferred_element_type=f32
    ).reshape(model_width, 3, head_cols)

    def qkv_term(row_start, count):
        return jnp.einsum("tk,dk->td", d_mixed_flat, qkv_flat, preferred_element_type=f32)

    d_norm1 = sum_tokens(qkv_term, local_rows)
    d_tokens_in, grad_gain1, grad_shift1 = norm1_back(d_norm1)
    grad_tokens = d_resid + d_tokens_in
    grad_wqkv = lax.psum_scatter(grad_wqkv, "row", scatter_dimension=0, tiled=True)
    grad_wout, grad_wdown, grad_wup = (
        lax.psum_scatter(grad_wout, "row", scatter_dimension=1, tiled=True),
        lax.psum_scatter(grad_wdown, "row", scatter_dimension=1, tiled=True),
        lax.psum_scatter(grad_wup, "row", scatter_dimension=1, tiled=True),
    )
    grad_bqv, grad_bup = lax.psum((grad_bqv, grad_bup), "row")
    grad_gain1, grad_shift1, grad_gain2, grad_shift2, grad_bout, grad_bdown = lax.psum(
        (grad_gain1, grad_shift1, grad_gain2, grad_shift2, grad_bout, grad_bdown), ("row", "col")
    )
    return (
        output,
        grad_tokens,
        grad_wqkv,
        grad_bqv,
        grad_wout,
        grad_bout,
        grad_wup,
        grad_bup,
        grad_wdown,
        grad_bdown,
        grad_gain1,
        grad_shift1,
        grad_gain2,
        grad_shift2,
    )


def solution(mesh):
    return jax.shard_map(
        body,
        mesh=mesh,
        in_specs=(
            P(("row", "col"), None),
            P(("row", "col")),
            P("row", None, "col"),
            P(None, "col"),
            P("col", "row"),
            P(),
            P("col", "row"),
            P("col"),
            P("col", "row"),
            P(),
            P(),
            P(),
            P(),
            P(),
            P(("row", "col"), None),
        ),
        out_specs=(
            P(("row", "col"), None),
            P(("row", "col"), None),
            P("row", None, "col"),
            P(None, "col"),
            P("col", "row"),
            P(),
            P("col", "row"),
            P("col"),
            P("col", "row"),
            P(),
            P(),
            P(),
            P(),
            P(),
        ),
        check_vma=False,
    )
```

profile of v0, /device:TPU:0, one launch (start us, length us, event | category | flops | bytes accessed | tf_op | source)
XLA Modules:
  0.0 1738.0 jit_solution(14940055284473691748)
XLA Ops:
  15.6 12.7 all_gather.29
  28.6 13.3 all-gather
  53.5 46.9 %all-gather.8.cloned.1.call-done = bf16[4096,1024]{1,0:T(8,128)(2,1)} async-done(((bf16[512,1024]{1,0:T(8,128)(2,1)}), bf16[4096,1024]{1,0:T(8,128)(2,1)}) %all-gather.8.cloned.1.call-update) | async-done | bytes 8388624 | tf_op jit(solution)/shard_map/all_gather | solution.py:74
  107.3 127.8 %while.29 = (s32[]{:T(128)}, bf16[8,512,2,64]{1,3,2,0:T(8,128)(2,1)}, f32[8,2,512,1]{2,1,3,0:T(2,128)S(1)}, s32[8]{0:T(128)S(1)}, s32[4096]{0:T(1024)S(1)}, /*in...) while((s32[]{:T(128)}, ...), condition=%wide.region_5.6_spmd.clone, body=%wide.region_2.5_spmd.sunk.clone | while | flops 1121975296 | bytes 61266096 | solution.py:107
  247.0 166.2 %reduce-scatter.9.cloned.1.call-done = f32[512,1024]{1,0:T(8,128)} async-done(((f32[4096,1024]{1,0:T(8,128)}), f32[512,1024]{1,0:T(8,128)}) %reduce-scatter.9.cloned.1.call-update) | async-done | bytes 2097168 | tf_op jit(solution)/shard_map/reduce_scatter | solution.py:110
  418.7 78.9 %all-gather.10.cloned.1.call-done = bf16[4096,1024]{1,0:T(8,128)(2,1)} async-done(((bf16[512,1024]{1,0:T(8,128)(2,1)}), bf16[4096,1024]{1,0:T(8,128)(2,1)}) %all-gather.10.cloned.1.call-update) | async-done | bytes 8388624 | tf_op jit(solution)/shard_map/all_gather | solution.py:23
  509.0 15.2 all-gather.14.cloned.1.call-done
  524.1 83.6 %all-gather.16.cloned.1.call-done = bf16[4096,1024]{1,0:T(8,128)(2,1)} async-done(((bf16[512,1024]{1,0:T(8,128)(2,1)}), bf16[4096,1024]{1,0:T(8,128)(2,1)}) %all-gather.16.cloned.1.call-update) | async-done | bytes 8388624 | tf_op jit(solution)/shard_map/all_gather | solution.py:23
  607.7 14.8 fusion.71
  632.9 12.6 convolution_convert_fusion
  646.1 153.2 %reduce-scatter.13.cloned.1.call-done = f32[512,1024]{1,0:T(8,128)} async-done(((f32[4096,1024]{1,0:T(8,128)}), f32[512,1024]{1,0:T(8,128)}) %reduce-scatter.13.cloned.1.call-update) | async-done | bytes 2097168 | tf_op jit(solution)/shard_map/reduce_scatter | solution.py:27
  802.2 87.3 %reduce-scatter.11.cloned.1.call-done = bf16[512,1024]{1,0:T(8,128)(2,1)} async-done(((bf16[4096,1024]{1,0:T(8,128)(2,1)}), bf16[512,1024]{1,0:T(8,128)(2,1)}) %reduce-scatter.11.cloned.1.call-update) | async-done | bytes 1048592 | tf_op jit(solution)/shard_map/reduce_scatter | solution.py:127
  896.0 80.6 %all-gather.18.cloned.1.call-done = bf16[4096,1024]{1,0:T(8,128)(2,1)} async-done(((bf16[512,1024]{1,0:T(8,128)(2,1)}), bf16[4096,1024]{1,0:T(8,128)(2,1)}) %all-gather.18.cloned.1.call-update) | async-done | bytes 8388624 | tf_op jit(solution)/shard_map/all_gather | solution.py:23
  983.8 418.1 %while.30 = (s32[]{:T(128)}, f32[4096,2,64]{0,2,1:T(8,128)S(1)}, f32[4096,2,64]{0,2,1:T(8,128)}, f32[8,512,2,64]{1,3,2,0:T(8,128)}, s32[8]{0:T(128)S(1)}, /*inde...) while((s32[]{:T(128)}, f32[4096,2,64]{0,2,1:T(8,128)S(1)}, ...), condition=%wide.region_15.16_spmd.clone.clone, body=%wide.region_13.15_spmd.clone.sunk.clone | while | flops 2752052224 | bytes 217893168 | solution.py:188
  1005.0 12.7 multiply_reduce_fusion.6
  1017.7 12.3 multiply_convert_fusion.6
  1057.3 12.6 multiply_reduce_fusion.6
  1069.9 12.3 multiply_convert_fusion.6
  1109.5 12.7 multiply_reduce_fusion.6
  1161.8 12.6 multiply_reduce_fusion.6
  1174.4 12.3 multiply_convert_fusion.6
  1214.0 12.6 multiply_reduce_fusion.6
  1266.3 12.7 multiply_reduce_fusion.6
  1278.9 12.3 multiply_convert_fusion.6
  1318.5 12.7 multiply_reduce_fusion.6
  1370.8 12.7 multiply_reduce_fusion.6
  1383.4 12.3 multiply_convert_fusion.6
  1481.4 109.7 %reduce-scatter.15.cloned.1.call-done = f32[512,1024]{1,0:T(8,128)} async-done(((f32[4096,1024]{1,0:T(8,128)}), f32[512,1024]{1,0:T(8,128)}) %reduce-scatter.15.cloned.1.call-update) | async-done | bytes 2097168 | tf_op jit(solution)/shard_map/reduce_scatter | solution.py:27
  1596.8 38.7 %all-reduce = (f32[1024]{0:T(1024)}, f32[1024]{0:T(1024)}, f32[1024]{0:T(1024)}, f32[1024]{0:T(1024)}, f32[1024]{0:T(1024)}, /*index=5*/f32[1024]{0:T(1024)}) all-reduce(f32[1024]{0:T(1024)S(1)} %get-tuple-element.165, f32[1024]{0:T(1024)S(1)} %get-tuple-element.164, ...), channel_id=1, replica_groups=mesh['row'=4,'col'=8] {'row','col'}, use_global_device_ids=true, to_apply=%region_25.26 | all-reduce | flops 6144 | bytes 49152 | tf_op jit(solution)/shard_map/psum | solution.py:214
  1635.5 31.8 %reduce-scatter.23.cloned.1.call-done = f32[512,256]{1,0:T(8,128)} async-done(((f32[512,1024]{1,0:T(8,128)}), f32[512,256]{1,0:T(8,128)}) %reduce-scatter.23.cloned.1.call-update) | async-done | bytes 524304 | tf_op jit(solution)/shard_map/reduce_scatter | solution.py:210
  1667.4 28.2 %reduce-scatter.19.cloned.1.call-done = f32[128,256]{1,0:T(8,128)} async-done(((f32[128,1024]{1,0:T(8,128)}), f32[128,256]{1,0:T(8,128)}) %reduce-scatter.19.cloned.1.call-update) | async-done | bytes 131088 | tf_op jit(solution)/shard_map/reduce_scatter | solution.py:209
  1695.6 34.8 %reduce-scatter.17.cloned.1.call-done = f32[256,3,128]{2,0,1:T(8,128)} async-done(((f32[1024,3,128]{2,0,1:T(8,128)}), f32[256,3,128]{2,0,1:T(8,128)}) %reduce-scatter.17.cloned.1.call-update) | async-done | bytes 393232 | tf_op jit(solution)/shard_map/reduce_scatter | solution.py:207
  (328 shorter events, 523.2 us)
Async XLA Ops:
  8.0 20.5 %copy-start.28 = (s32[512]{0:T(512)S(1)}, s32[512]{0:T(512)}, u32[]{:S(2)}) copy-start(s32[512]{0:T(512)} %param.20) | copy-start | bytes 6148
  8.0 33.8 %copy-start.19 = (bf16[128,256]{1,0:T(8,128)(2,1)S(1)}, bf16[128,256]{1,0:T(8,128)(2,1)}, u32[]{:S(2)}) copy-start(bf16[128,256]{1,0:T(8,128)(2,1)} %param.23) | copy-start | bytes 196612
  8.1 92.3 %all-gather.8.cloned.1.call-start = ((), (), s32[]{:S(2)}) async-start(), calls=%async_computation.8 | async-start | bytes 9437184 | tf_op jit(solution)/shard_map/all_gather | solution.py:74
  15.3 397.9 %reduce-scatter.9.cloned.1.call-start = ((), (), s32[]{:S(2)}) async-start(), calls=%async_computation.9 | async-start | bytes 18874368 | tf_op jit(solution)/shard_map/reduce_scatter | solution.py:110
  28.3 78.0 %copy-start.12 = (bf16[1024,3,128]{2,0,1:T(8,128)(2,1)}, bf16[1024,3,128]{2,0,1:T(8,128)(2,1)S(1)}, u32[]{:S(2)}) copy-start(bf16[1024,3,128]{2,0,1:T(8,128)(2,1)S(1)} %all_gather.29) | copy-start | bytes 2359300
  235.2 11.1 copy-start.2
  238.1 8.1 copy-start.7
  246.3 172.4 %all-gather.12.cloned.1.call-start = ((), (), s32[]{:S(2)}) async-start(), calls=%async_computation.11 | async-start | bytes 1310720 | tf_op jit(solution)/shard_map/all_gather | solution.py:68
  246.9 250.7 %all-gather.10.cloned.1.call-start = ((), (), s32[]{:S(2)}) async-start(), calls=%async_computation.10 | async-start | bytes 9437184 | tf_op jit(solution)/shard_map/all_gather | solution.py:23
  417.2 106.9 %all-gather.14.cloned.1.call-start = ((), (), s32[]{:S(2)}) async-start(), calls=%async_computation.12 | async-start | bytes 1310720 | tf_op jit(solution)/shard_map/all_gather | solution.py:67
  417.8 189.9 %all-gather.16.cloned.1.call-start = ((), (), s32[]{:S(2)}) async-start(), calls=%async_computation.14 | async-start | bytes 9437184 | tf_op jit(solution)/shard_map/all_gather | solution.py:23
  418.5 380.7 %reduce-scatter.13.cloned.1.call-start = ((), (), s32[]{:S(2)}) async-start(), calls=%async_computation.15 | async-start | bytes 18874368 | tf_op jit(solution)/shard_map/reduce_scatter | solution.py:27
  418.6 214.3 %copy-start.34 = (f32[512]{0:T(512)}, f32[512]{0:T(512)S(1)}, u32[]{:S(2)}) copy-start(f32[512]{0:T(512)S(1)} %convert_element_type.106) | copy-start | bytes 6148
  607.7 16.8 copy-start.37
  632.6 256.9 %reduce-scatter.11.cloned.1.call-start = ((), (), s32[]{:S(2)}) async-start(), calls=%async_computation.13 | async-start | bytes 9437184 | tf_op jit(solution)/shard_map/reduce_scatter | solution.py:127
  645.5 331.1 %all-gather.18.cloned.1.call-start = ((), (), s32[]{:S(2)}) async-start(), calls=%async_computation.16 | async-start | bytes 9437184 | tf_op jit(solution)/shard_map/all_gather | solution.py:23
  895.9 695.2 %reduce-scatter.15.cloned.1.call-start = ((), (), s32[]{:S(2)}) async-start(), calls=%async_computation.17 | async-start | bytes 18874368 | tf_op jit(solution)/shard_map/reduce_scatter | solution.py:27
  1258.6 7.6 copy-start.3
  1310.9 7.6 copy-start.3
  1424.2 10.9 copy-start.35
  1424.2 211.4 %reduce-scatter.21.cloned.1.call-start = ((), (), s32[]{:S(2)}) async-start(), calls=%async_computation.20 | async-start | bytes 2621440 | tf_op jit(solution)/shard_map/reduce_scatter | solution.py:211
  1434.8 232.5 %reduce-scatter.23.cloned.1.call-start = ((), (), s32[]{:S(2)}) async-start(), calls=%async_computation.21 | async-start | bytes 2621440 | tf_op jit(solution)/shard_map/reduce_scatter | solution.py:210
  1447.1 248.5 %reduce-scatter.19.cloned.1.call-start = ((), (), s32[]{:S(2)}) async-start(), calls=%async_computation.19 | async-start | bytes 655360 | tf_op jit(solution)/shard_map/reduce_scatter | solution.py:209
  1459.5 9.2 copy-start.11
  1459.5 270.8 %reduce-scatter.17.cloned.1.call-start = ((), (), s32[]{:S(2)}) async-start(), calls=%async_computation.18 | async-start | bytes 1966080 | tf_op jit(solution)/shard_map/reduce_scatter | solution.py:207
  1468.6 122.5 %copy-start.1 = (bf16[512,1024]{1,0:T(8,128)(2,1)S(1)}, bf16[512,1024]{1,0:T(8,128)(2,1)}, u32[]{:S(2)}) copy-start(bf16[512,1024]{1,0:T(8,128)(2,1)} %param.19) | copy-start | bytes 3145732
  1468.6 122.5 %copy-start.16 = (f32[1024]{0:T(1024)S(1)}, f32[1024]{0:T(1024)}, u32[]{:S(2)}) copy-start(f32[1024]{0:T(1024)} %copy-done.15) | copy-start | bytes 12292
  1468.6 122.5 %copy-start.18 = (f32[512]{0:T(512)S(1)}, f32[512]{0:T(512)}, u32[]{:S(2)}) copy-start(f32[512]{0:T(512)} %copy-done.17) | copy-start | bytes 6148
  1468.6 124.8 %copy-start.25 = (f32[512]{0:T(512)S(1)}, f32[512]{0:T(512)}, u32[]{:S(2)}) copy-start(f32[512]{0:T(512)} %copy-done.24) | copy-start | bytes 6148
  1468.7 124.8 %copy-start.21 = (f32[512]{0:T(512)S(1)}, f32[512]{0:T(512)}, u32[]{:S(2)}) copy-start(f32[512]{0:T(512)} %copy-done.20) | copy-start | bytes 6148
  1468.9 125.6 %copy-start.6 = (f32[512,1024]{1,0:T(8,128)S(1)}, f32[512,1024]{1,0:T(8,128)}, u32[]{:S(2)}) copy-start(f32[512,1024]{1,0:T(8,128)} %copy-done.5) | copy-start | bytes 6291460
  1468.9 125.6 %copy-start.23 = (f32[512]{0:T(512)S(1)}, f32[512]{0:T(512)}, u32[]{:S(2)}) copy-start(f32[512]{0:T(512)} %copy-done.22) | copy-start | bytes 6148
  (36 other events, 154.3 us)
Sparse Core Ops, SparseCore 0:
  15.5 84.8 all-gather.7
  246.4 166.7 reduce-scatter.8
  896.0 80.5 all-gather.17
  1424.3 166.7 reduce-scatter.14
  1594.5 33.9 reduce-scatter.20
  1632.1 35.1 reduce-scatter.22
  1670.8 24.7 reduce-scatter.18
  1699.4 30.9 reduce-scatter.16
Sparse Core Ops, SparseCore 1:
  248.6 24.8 all-gather.11
  417.3 80.2 all-gather.9
  499.3 24.8 all-gather.13
  525.8 81.9 all-gather.15
  632.7 166.5 reduce-scatter.12
  801.6 87.8 reduce-scatter.10
where the time goes:
time: 1740 us
  waiting for transfers between devices  918 us (53%)
  matrix products  421 us (24%)
  other arithmetic  186 us (11%)
  blocking collectives  85.6 us (5%)
  local copies, waits for them, and re-layouts  82.3 us (5%)
  loops' own time  27.5 us (2%)
    reduce_scatter x2, waiting for transfers between devices, sum_tokens(): lax.psum_scatter(term_fn(jnp.int32(0), lax.axis_size('col') * local_rows)...  263 us
    all_gather x3, waiting for transfers between devices, gather_tokens(): return lax.all_gather(rows_in, 'col', axis=0, tiled=True)  243 us
    reduce_scatter x1, waiting for transfers between devices, body(): lax.psum_scatter(jnp.dot(part, out_weight, preferred_element_type=f32), '...  166 us
    dot_general x8, matrix products, backward_block(): jnp.einsum('qhd,khd->hqk', dout_part, value_seq, preferred_element_type=f32)  101 us
    convert_element_type x8, other arithmetic, backward_block(): d_scores_low = d_scores.astype(bf16)  98.2 us
    reduce_scatter x1, waiting for transfers between devices, body(): lax.psum_scatter(jnp.dot(part, down_all, preferred_element_type=f32).asty...  87.3 us
    dot_general x8, matrix products, backward_block(): jnp.einsum('hqk,qhd->khd', probs_low, dout_part, preferred_element_type=f32)  60.6 us
    dot_general x16, matrix products, block_scores(): jnp.einsum('qhd,khd->hqk', query_part, key_seq, preferred_element_type=f32)  56.1 us
  transfers between devices with their start and end apart: 14, of which 12 were waited for; matrix products, arithmetic and copies ran while one was open for 5% of the time, Pallas kernels for 0%

commit v1 on v0

--- a/solution.py
+++ b/solution.py
@@ -212,7 +212,8 @@
     )
     grad_bqv, grad_bup = lax.psum((grad_bqv, grad_bup), "row")
     grad_gain1, grad_shift1, grad_gain2, grad_shift2, grad_bout, grad_bdown = lax.psum(
-        (grad_gain1, grad_shift1, grad_gain2, grad_shift2, grad_bout, grad_bdown), ("row", "col")
+        lax.psum((grad_gain1, grad_shift1, grad_gain2, grad_shift2, grad_bout, grad_bdown), "col"),
+        "row",
     )
     return (
         output,

time: 1740 us -> 1740 us (level)
  no operation moved by 1% of the time
where the time goes in v1:
time: 1740 us
  waiting for transfers between devices  925 us (53%)
  matrix products  421 us (24%)
  other arithmetic  186 us (11%)
  local copies, waits for them, and re-layouts  82.2 us (5%)
  blocking collectives  79.3 us (5%)
  loops' own time  27.5 us (2%)
    reduce_scatter x2, waiting for transfers between devices, sum_tokens(): lax.psum_scatter(term_fn(jnp.int32(0), lax.axis_size('col') * local_rows)...  273 us
    all_gather x3, waiting for transfers between devices, gather_tokens(): return lax.all_gather(rows_in, 'col', axis=0, tiled=True)  243 us
    reduce_scatter x1, waiting for transfers between devices, body(): lax.psum_scatter(jnp.dot(part, out_weight, preferred_element_type=f32), '...  166 us
    dot_general x8, matrix products, backward_block(): jnp.einsum('qhd,khd->hqk', dout_part, value_seq, preferred_element_type=f32)  101 us
    convert_element_type x8, other arithmetic, backward_block(): d_scores_low = d_scores.astype(bf16)  98.2 us
    reduce_scatter x1, waiting for transfers between devices, body(): lax.psum_scatter(jnp.dot(part, down_all, preferred_element_type=f32).asty...  87.3 us
    dot_general x8, matrix products, backward_block(): jnp.einsum('hqk,qhd->khd', probs_low, dout_part, preferred_element_type=f32)  60.6 us
    dot_general x16, matrix products, block_scores(): jnp.einsum('qhd,khd->hqk', query_part, key_seq, preferred_element_type=f32)  56.2 us
  transfers between devices with their start and end apart: 14, of which 12 were waited for; matrix products, arithmetic and copies ran while one was open for 5% of the time, Pallas kernels for 0%

profile of v1, /device:TPU:0, one launch (start us, length us, event | category | flops | bytes accessed | tf_op | source)
XLA Modules:
  0.0 1738.0 jit_solution(1961966382327832416)
XLA Ops:
  15.6 12.7 all_gather.29
  28.6 13.3 all-gather
  53.5 46.9 %all-gather.8.cloned.1.call-done = bf16[4096,1024]{1,0:T(8,128)(2,1)} async-done(((bf16[512,1024]{1,0:T(8,128)(2,1)}), bf16[4096,1024]{1,0:T(8,128)(2,1)}) %all-gather.8.cloned.1.call-update) | async-done | bytes 8388624 | tf_op jit(solution)/shard_map/all_gather | solution.py:74
  107.3 127.8 %while.29 = (s32[]{:T(128)}, bf16[8,512,2,64]{1,3,2,0:T(8,128)(2,1)}, f32[8,2,512,1]{2,1,3,0:T(2,128)S(1)}, s32[8]{0:T(128)S(1)}, s32[4096]{0:T(1024)S(1)}, /*in...) while((s32[]{:T(128)}, ...), condition=%wide.region_5.6_spmd.clone, body=%wide.region_2.5_spmd.sunk.clone | while | flops 1121975296 | bytes 61266096 | solution.py:107
  247.0 166.2 %reduce-scatter.9.cloned.1.call-done = f32[512,1024]{1,0:T(8,128)} async-done(((f32[4096,1024]{1,0:T(8,128)}), f32[512,1024]{1,0:T(8,128)}) %reduce-scatter.9.cloned.1.call-update) | async-done | bytes 2097168 | tf_op jit(solution)/shard_map/reduce_scatter | solution.py:110
  418.7 78.9 %all-gather.10.cloned.1.call-done = bf16[4096,1024]{1,0:T(8,128)(2,1)} async-done(((bf16[512,1024]{1,0:T(8,128)(2,1)}), bf16[4096,1024]{1,0:T(8,128)(2,1)}) %all-gather.10.cloned.1.call-update) | async-done | bytes 8388624 | tf_op jit(solution)/shard_map/all_gather | solution.py:23
  509.0 15.2 all-gather.14.cloned.1.call-done
  524.1 83.6 %all-gather.16.cloned.1.call-done = bf16[4096,1024]{1,0:T(8,128)(2,1)} async-done(((bf16[512,1024]{1,0:T(8,128)(2,1)}), bf16[4096,1024]{1,0:T(8,128)(2,1)}) %all-gather.16.cloned.1.call-update) | async-done | bytes 8388624 | tf_op jit(solution)/shard_map/all_gather | solution.py:23
  607.7 14.8 fusion.71
  632.9 12.6 convolution_convert_fusion
  646.1 153.2 %reduce-scatter.13.cloned.1.call-done = f32[512,1024]{1,0:T(8,128)} async-done(((f32[4096,1024]{1,0:T(8,128)}), f32[512,1024]{1,0:T(8,128)}) %reduce-scatter.13.cloned.1.call-update) | async-done | bytes 2097168 | tf_op jit(solution)/shard_map/reduce_scatter | solution.py:27
  802.2 87.3 %reduce-scatter.11.cloned.1.call-done = bf16[512,1024]{1,0:T(8,128)(2,1)} async-done(((bf16[4096,1024]{1,0:T(8,128)(2,1)}), bf16[512,1024]{1,0:T(8,128)(2,1)}) %reduce-scatter.11.cloned.1.call-update) | async-done | bytes 1048592 | tf_op jit(solution)/shard_map/reduce_scatter | solution.py:127
  896.0 80.6 %all-gather.18.cloned.1.call-done = bf16[4096,1024]{1,0:T(8,128)(2,1)} async-done(((bf16[512,1024]{1,0:T(8,128)(2,1)}), bf16[4096,1024]{1,0:T(8,128)(2,1)}) %all-gather.18.cloned.1.call-update) | async-done | bytes 8388624 | tf_op jit(solution)/shard_map/all_gather | solution.py:23
  983.8 418.2 %while.30 = (s32[]{:T(128)}, f32[4096,2,64]{0,2,1:T(8,128)S(1)}, f32[4096,2,64]{0,2,1:T(8,128)}, f32[8,512,2,64]{1,3,2,0:T(8,128)}, s32[8]{0:T(128)S(1)}, /*inde...) while((s32[]{:T(128)}, f32[4096,2,64]{0,2,1:T(8,128)S(1)}, ...), condition=%wide.region_15.16_spmd.clone.clone, body=%wide.region_13.15_spmd.clone.sunk.clone | while | flops 2752052224 | bytes 217893168 | solution.py:188
  1005.0 12.7 multiply_reduce_fusion.6
  1057.3 12.6 multiply_reduce_fusion.6
  1069.9 12.3 multiply_convert_fusion.6
  1109.5 12.7 multiply_reduce_fusion.6
  1161.8 12.6 multiply_reduce_fusion.6
  1174.4 12.3 multiply_convert_fusion.6
  1214.0 12.6 multiply_reduce_fusion.6
  1266.3 12.7 multiply_reduce_fusion.6
  1278.9 12.3 multiply_convert_fusion.6
  1318.5 12.7 multiply_reduce_fusion.6
  1370.8 12.7 multiply_reduce_fusion.6
  1383.4 12.3 multiply_convert_fusion.6
  1471.0 120.1 %reduce-scatter.15.cloned.1.call-done = f32[512,1024]{1,0:T(8,128)} async-done(((f32[4096,1024]{1,0:T(8,128)}), f32[512,1024]{1,0:T(8,128)}) %reduce-scatter.15.cloned.1.call-update) | async-done | bytes 2097168 | tf_op jit(solution)/shard_map/reduce_scatter | solution.py:27
  1596.8 26.0 %all-reduce = (f32[1024]{0:T(1024)S(1)}, f32[1024]{0:T(1024)S(1)}, f32[1024]{0:T(1024)S(1)}, f32[1024]{0:T(1024)S(1)}, f32[1024]{0:T(1024)S(1)}, /*index=5*/f32[1024]{0:T(1024)S(1)}) all-reduce(f32[1024]{0:T(1024)S(1)} %get-tuple-element.165, f32[1024]{0:T(1024)S(1)} %get-tuple-element.164, ...), channel_id=1, replica_groups=mesh['row'=4,'col'=8] {'col'}, use_global_device_ids=true, to_apply=%region_25.26 | all-reduce | flops 6144 | bytes 49152 | tf_op jit(solution)/shard_map/psum | solution.py:215
  1622.8 16.8 all-reduce.1
  1639.6 27.8 %reduce-scatter.23.cloned.1.call-done = f32[512,256]{1,0:T(8,128)} async-done(((f32[512,1024]{1,0:T(8,128)}), f32[512,256]{1,0:T(8,128)}) %reduce-scatter.23.cloned.1.call-update) | async-done | bytes 524304 | tf_op jit(solution)/shard_map/reduce_scatter | solution.py:210
  1667.4 28.2 %reduce-scatter.19.cloned.1.call-done = f32[128,256]{1,0:T(8,128)} async-done(((f32[128,1024]{1,0:T(8,128)}), f32[128,256]{1,0:T(8,128)}) %reduce-scatter.19.cloned.1.call-update) | async-done | bytes 131088 | tf_op jit(solution)/shard_map/reduce_scatter | solution.py:209
  1695.6 34.8 %reduce-scatter.17.cloned.1.call-done = f32[256,3,128]{2,0,1:T(8,128)} async-done(((f32[1024,3,128]{2,0,1:T(8,128)}), f32[256,3,128]{2,0,1:T(8,128)}) %reduce-scatter.17.cloned.1.call-update) | async-done | bytes 393232 | tf_op jit(solution)/shard_map/reduce_scatter | solution.py:207
  (328 shorter events, 525.1 us)
Async XLA Ops:
  8.0 20.5 %copy-start.28 = (s32[512]{0:T(512)S(1)}, s32[512]{0:T(512)}, u32[]{:S(2)}) copy-start(s32[512]{0:T(512)} %param.20) | copy-start | bytes 6148
  8.0 33.8 %copy-start.19 = (bf16[128,256]{1,0:T(8,128)(2,1)S(1)}, bf16[128,256]{1,0:T(8,128)(2,1)}, u32[]{:S(2)}) copy-start(bf16[128,256]{1,0:T(8,128)(2,1)} %param.23) | copy-start | bytes 196612
  8.1 92.3 %all-gather.8.cloned.1.call-start = ((), (), s32[]{:S(2)}) async-start(), calls=%async_computation.8 | async-start | bytes 9437184 | tf_op jit(solution)/shard_map/all_gather | solution.py:74
  15.3 397.9 %reduce-scatter.9.cloned.1.call-start = ((), (), s32[]{:S(2)}) async-start(), calls=%async_computation.9 | async-start | bytes 18874368 | tf_op jit(solution)/shard_map/reduce_scatter | solution.py:110
  28.3 78.0 %copy-start.12 = (bf16[1024,3,128]{2,0,1:T(8,128)(2,1)}, bf16[1024,3,128]{2,0,1:T(8,128)(2,1)S(1)}, u32[]{:S(2)}) copy-start(bf16[1024,3,128]{2,0,1:T(8,128)(2,1)S(1)} %all_gather.29) | copy-start | bytes 2359300
  235.2 11.1 copy-start.2
  238.1 8.1 copy-start.7
  246.3 172.4 %all-gather.12.cloned.1.call-start = ((), (), s32[]{:S(2)}) async-start(), calls=%async_computation.11 | async-start | bytes 1310720 | tf_op jit(solution)/shard_map/all_gather | solution.py:68
  246.9 250.7 %all-gather.10.cloned.1.call-start = ((), (), s32[]{:S(2)}) async-start(), calls=%async_computation.10 | async-start | bytes 9437184 | tf_op jit(solution)/shard_map/all_gather | solution.py:23
  417.2 106.9 %all-gather.14.cloned.1.call-start = ((), (), s32[]{:S(2)}) async-start(), calls=%async_computation.12 | async-start | bytes 1310720 | tf_op jit(solution)/shard_map/all_gather | solution.py:67
  417.8 189.9 %all-gather.16.cloned.1.call-start = ((), (), s32[]{:S(2)}) async-start(), calls=%async_computation.14 | async-start | bytes 9437184 | tf_op jit(solution)/shard_map/all_gather | solution.py:23
  418.5 380.8 %reduce-scatter.13.cloned.1.call-start = ((), (), s32[]{:S(2)}) async-start(), calls=%async_computation.15 | async-start | bytes 18874368 | tf_op jit(solution)/shard_map/reduce_scatter | solution.py:27
  418.6 214.2 %copy-start.34 = (f32[512]{0:T(512)}, f32[512]{0:T(512)S(1)}, u32[]{:S(2)}) copy-start(f32[512]{0:T(512)S(1)} %convert_element_type.106) | copy-start | bytes 6148
  607.7 16.8 copy-start.37
  632.6 256.9 %reduce-scatter.11.cloned.1.call-start = ((), (), s32[]{:S(2)}) async-start(), calls=%async_computation.13 | async-start | bytes 9437184 | tf_op jit(solution)/shard_map/reduce_scatter | solution.py:127
  645.4 331.1 %all-gather.18.cloned.1.call-start = ((), (), s32[]{:S(2)}) async-start(), calls=%async_computation.16 | async-start | bytes 9437184 | tf_op jit(solution)/shard_map/all_gather | solution.py:23
  895.9 695.2 %reduce-scatter.15.cloned.1.call-start = ((), (), s32[]{:S(2)}) async-start(), calls=%async_computation.17 | async-start | bytes 18874368 | tf_op jit(solution)/shard_map/reduce_scatter | solution.py:27
  1310.9 7.6 copy-start.3
  1424.2 10.9 copy-start.35
  1424.2 215.4 %reduce-scatter.21.cloned.1.call-start = ((), (), s32[]{:S(2)}) async-start(), calls=%async_computation.20 | async-start | bytes 2621440 | tf_op jit(solution)/shard_map/reduce_scatter | solution.py:211
  1434.8 232.6 %reduce-scatter.23.cloned.1.call-start = ((), (), s32[]{:S(2)}) async-start(), calls=%async_computation.21 | async-start | bytes 2621440 | tf_op jit(solution)/shard_map/reduce_scatter | solution.py:210
  1447.1 248.5 %reduce-scatter.19.cloned.1.call-start = ((), (), s32[]{:S(2)}) async-start(), calls=%async_computation.19 | async-start | bytes 655360 | tf_op jit(solution)/shard_map/reduce_scatter | solution.py:209
  1459.5 9.2 copy-start.11
  1459.5 270.8 %reduce-scatter.17.cloned.1.call-start = ((), (), s32[]{:S(2)}) async-start(), calls=%async_computation.18 | async-start | bytes 1966080 | tf_op jit(solution)/shard_map/reduce_scatter | solution.py:207
  1468.6 122.5 %copy-start.1 = (bf16[512,1024]{1,0:T(8,128)(2,1)S(1)}, bf16[512,1024]{1,0:T(8,128)(2,1)}, u32[]{:S(2)}) copy-start(bf16[512,1024]{1,0:T(8,128)(2,1)} %param.19) | copy-start | bytes 3145732
  1468.6 122.5 %copy-start.16 = (f32[1024]{0:T(1024)S(1)}, f32[1024]{0:T(1024)}, u32[]{:S(2)}) copy-start(f32[1024]{0:T(1024)} %copy-done.15) | copy-start | bytes 12292
  1468.6 122.5 %copy-start.18 = (f32[512]{0:T(512)S(1)}, f32[512]{0:T(512)}, u32[]{:S(2)}) copy-start(f32[512]{0:T(512)} %copy-done.17) | copy-start | bytes 6148
  1468.6 124.8 %copy-start.25 = (f32[512]{0:T(512)S(1)}, f32[512]{0:T(512)}, u32[]{:S(2)}) copy-start(f32[512]{0:T(512)} %copy-done.24) | copy-start | bytes 6148
  1468.6 124.8 %copy-start.21 = (f32[512]{0:T(512)S(1)}, f32[512]{0:T(512)}, u32[]{:S(2)}) copy-start(f32[512]{0:T(512)} %copy-done.20) | copy-start | bytes 6148
  1468.9 125.6 %copy-start.6 = (f32[512,1024]{1,0:T(8,128)S(1)}, f32[512,1024]{1,0:T(8,128)}, u32[]{:S(2)}) copy-start(f32[512,1024]{1,0:T(8,128)} %copy-done.5) | copy-start | bytes 6291460
  1468.9 125.6 %copy-start.23 = (f32[512]{0:T(512)S(1)}, f32[512]{0:T(512)}, u32[]{:S(2)}) copy-start(f32[512]{0:T(512)} %copy-done.22) | copy-start | bytes 6148
  1594.5 28.3 %copy-start.33 = (f32[512]{0:T(512)S(1)}, f32[512]{0:T(512)}, u32[]{:S(2)}) copy-start(f32[512]{0:T(512)} %get-tuple-element.222) | copy-start | bytes 6148
  (36 other events, 159.5 us)
Sparse Core Ops, SparseCore 0:
  15.5 84.8 all-gather.7
  246.4 166.7 reduce-scatter.8
  896.0 80.4 all-gather.17
  1424.3 166.7 reduce-scatter.14
  1594.5 33.7 reduce-scatter.20
  1631.9 35.4 reduce-scatter.22
  1670.8 24.7 reduce-scatter.18
  1699.4 30.9 reduce-scatter.16
Sparse Core Ops, SparseCore 1:
  248.6 24.8 all-gather.11
  417.3 80.2 all-gather.9
  499.3 24.8 all-gather.13
  525.8 81.9 all-gather.15
  632.7 166.6 reduce-scatter.12
  801.6 87.8 reduce-scatter.10
